TPU v7x, 32 devices: a whole 2x2x4 slice. The times are simulated.
32 devices in a mesh: expert: 8 (over z, y), tensor: 4 (over x, core).
Axes of the slice: x: 2, y: 2, z: 4, core: 2. Of those that a mesh axis runs over, the one named last changes fastest.
Arguments:
- tokens: bfloat16 [1024, 7168], P('expert', 'tensor'), may hold values from -6 to 6
- out_grad: bfloat16 [1024, 7168], P('expert', 'tensor'), may hold values from -1.5 to 1.5
- expert_ids: int32 [1024, 2], P('expert'), may hold values from 0 to 7, all different within a row; in each aligned block of 128 rows (0 to 127, 128 to 255, ...) at most 48 rows name the same one
- gate_values: bfloat16 [1024, 2], P('expert'), may hold values from 0.099609375 to 1
- w_gate: bfloat16 [8, 7168, 1024], P('expert', None, 'tensor'), may hold values from -0.0625 to 0.0625
- w_up: bfloat16 [8, 7168, 1024], P('expert', None, 'tensor'), may hold values from -0.0625 to 0.0625
- w_down: bfloat16 [8, 1024, 7168], P('expert', 'tensor'), may hold values from -0.1875 to 0.1875
Outputs:
- d_tokens: bfloat16 [1024, 7168], P('expert', 'tensor')
- d_gates: float32 [1024, 2], P('expert')
Inputs may be any that keep to these rules, and one draw needn't show every extreme that they name: `expert_ids`: each row names 2 different experts. Among the 128 rows held at one index along `expert` (one aligned block) no expert is named by more than 48 rows, and in some such block one expert is named by exactly 48.
All inputs are finite; a program needn't handle non-finite values.
Results may differ from a plain program's by a relative error of at most 0.0049.
Values may be sent and summed in bfloat16 or wider, within the bound.
A program may use at most 128 MiB of HBM per device.

v0:
```python
import jax
import jax.numpy as jnp
from jax import lax
from jax.sharding import PartitionSpec as P


def local(tokens, out_grad, expert_ids, gate_values, w_gate, w_up, w_down):
    n_experts = lax.axis_size("expert")
    tok_rows, quarter = tokens.shape
    top_count = expert_ids.shape[1]
    most_slots = 3 * tok_rows * top_count // (2 * n_experts)
    slot_count = n_experts * most_slots
    flat_ids = expert_ids.reshape(-1)
    onehot = (flat_ids[:, None] == jnp.arange(n_experts, dtype=jnp.int32)[None, :]).astype(
        jnp.int32
    )
    before = jnp.cumsum(onehot, axis=0) - onehot
    rank = jnp.sum(before * onehot, axis=1)
    slot_of = (flat_ids * most_slots + rank).reshape(tok_rows, top_count)
    matches = slot_of[None, :, :] == jnp.arange(slot_count, dtype=jnp.int32)[:, None, None]
    chooser = jnp.any(matches, axis=2).astype(jnp.bfloat16)
    send_x = jnp.dot(chooser, tokens, preferred_element_type=jnp.float32).astype(jnp.bfloat16)
    send_dy = jnp.dot(chooser, out_grad, preferred_element_type=jnp.float32).astype(jnp.bfloat16)
    gate_wide = gate_values.astype(jnp.float32)[None, :, :]
    send_g = jnp.sum(jnp.where(matches, gate_wide, 0.0), axis=(1, 2)).astype(jnp.bfloat16)
    recv_x, recv_dy, recv_g = (
        lax.all_to_all(
            send_x.reshape(n_experts, most_slots, quarter),
            "expert",
            split_axis=0,
            concat_axis=0,
            tiled=True,
        ),
        lax.all_to_all(
            send_dy.reshape(n_experts, most_slots, quarter),
            "expert",
            split_axis=0,
            concat_axis=0,
            tiled=True,
        ),
        lax.all_to_all(
            send_g.reshape(n_experts, most_slots), "expert", split_axis=0, concat_axis=0, tiled=True
        ),
    )
    rows_x = recv_x.reshape(slot_count, quarter)
    rows_dy = recv_dy.reshape(slot_count, quarter)
    gate_mat = w_gate[0]
    up_mat = w_up[0]
    down_mat = w_down[0]
    piece_x = lax.all_gather(rows_x, "tensor", axis=1, tiled=True)
    piece_dy = lax.all_gather(rows_dy, "tensor", axis=1, tiled=True)
    pre_sum = jnp.dot(piece_x, gate_mat, preferred_element_type=jnp.float32)
    up_sum = jnp.dot(piece_x, up_mat, preferred_element_type=jnp.float32)
    grad_sum = lax.dot_general(
        piece_dy, down_mat, (((1,), (1,)), ((), ())), preferred_element_type=jnp.float32
    )
    sigma = jax.nn.sigmoid(pre_sum)
    active = pre_sum * sigma
    partial_grad = jnp.sum(active * up_sum * grad_sum, axis=1)
    weight_g = recv_g.reshape(slot_count).astype(jnp.float32)
    scaled = weight_g[:, None] * grad_sum
    grad_up = (scaled * active).astype(jnp.bfloat16)
    grad_pre = (scaled * up_sum * sigma * (1.0 + pre_sum * (1.0 - sigma))).astype(jnp.bfloat16)
    contrib = lax.dot_general(
        grad_pre, gate_mat, (((1,), (1,)), ((), ())), preferred_element_type=jnp.float32
    )
    contrib = contrib + lax.dot_general(
        grad_up, up_mat, (((1,), (1,)), ((), ())), preferred_element_type=jnp.float32
    )
    slot_grad = lax.psum(partial_grad, "tensor")
    shares = lax.psum_scatter(
        contrib.astype(jnp.bfloat16), "tensor", scatter_dimension=1, tiled=True
    )
    returned = lax.all_to_all(
        shares.reshape(n_experts, most_slots, quarter),
        "expert",
        split_axis=0,
        concat_axis=0,
        tiled=True,
    )
    returned_grad = lax.all_to_all(
        slot_grad.reshape(n_experts, most_slots), "expert", split_axis=0, concat_axis=0, tiled=True
    )
    d_tokens = lax.dot_general(
        chooser,
        returned.reshape(slot_count, quarter),
        (((0,), (0,)), ((), ())),
        preferred_element_type=jnp.float32,
    ).astype(jnp.bfloat16)
    grad_wide = returned_grad.reshape(slot_count)[:, None, None]
    d_gates = jnp.sum(jnp.where(matches, grad_wide, 0.0), axis=0)
    return (d_tokens, d_gates)


def solution(mesh):
    placed = (
        P("expert", "tensor"),
        P("expert", "tensor"),
        P("expert", None),
        P("expert", None),
        P("expert", None, "tensor"),
        P("expert", None, "tensor"),
        P("expert", "tensor", None),
    )
    return jax.shard_map(
        local,
        mesh=mesh,
        in_specs=placed,
        out_specs=(P("expert", "tensor"), P("expert", None)),
        check_vma=False,
    )
```

profile of v0, /device:TPU:0, one launch (start us, length us, event | category | flops | bytes accessed | tf_op | source)
XLA Modules:
  0.0 276.1 jit_solution(810567907580985810)
XLA Ops:
  7.2 0.0 copy-start
  7.2 0.0 copy-start.3
  7.2 0.0 all-gather.5.cloned.1.call-start
  7.2 0.9 copy.28
  8.1 0.1 eq.42
  8.2 0.1 eq.38
  8.4 0.6 reduce-window.6
  9.0 0.2 slice_reduce_fusion
  9.2 0.1 fusion.16
  9.3 0.1 reduce_sum.39
  9.5 0.1 copy.30
  9.5 0.7 multiply_add_fusion
  10.3 0.0 copy-done
  10.3 0.5 convolution_convert_fusion
  10.8 40.6 %all_to_all.30 = bf16[8,48,1792]{2,1,0:T(8,128)(2,1)} all-to-all(bf16[8,48,1792]{2,1,0:T(8,128)(2,1)S(1)} %bitcast.41), channel_id=1, replica_groups=mesh['expert'=8,'tensor'=4] {'expert'}, dimensions={0} | all-to-all | bytes 2752512 | tf_op jit(solution)/shard_map/all_to_all | solution.py:27
  51.4 0.0 all-gather.5.cloned.1.call-update
  51.4 0.0 all-gather.3.cloned.1.call-start
  51.5 0.0 copy-done.3
  51.5 0.5 convolution_convert_fusion.1
  52.0 36.1 %all_to_all.31 = bf16[8,48,1792]{2,1,0:T(8,128)(2,1)} all-to-all(bf16[8,48,1792]{2,1,0:T(8,128)(2,1)S(1)} %bitcast.42), channel_id=1, replica_groups=mesh['expert'=8,'tensor'=4] {'expert'}, dimensions={0} | all-to-all | bytes 2752512 | tf_op jit(solution)/shard_map/all_to_all | solution.py:34
  88.1 0.0 all-gather.3.cloned.1.call-update
  88.2 3.7 %all-gather.5.cloned.1.call-done = bf16[384,7168]{1,0:T(8,128)(2,1)} async-done(((bf16[384,1792]{1,0:T(8,128)(2,1)}), bf16[384,7168]{1,0:T(8,128)(2,1)}) %all-gather.5.cloned.1.call-update) | async-done | bytes 5505040 | tf_op jit(solution)/shard_map/all_gather | solution.py:50
  91.9 5.9 %fusion.2 = f32[384,256]{0,1:T(8,128)S(1)} fusion(bf16[384,7168]{1,0:T(8,128)(2,1)} %all-gather.5.cloned.1.call-done, bf16[1,7168,256]{2,1,0:T(8,128)(2,1)} %param.11), kind=kOutput, calls=%fused_computation.3 | convolution fusion | flops 1409286144 | bytes 9568256 | tf_op jit(solution)/shard_map/dot_general | solution.py:52
  97.8 0.0 copy-done.1
  97.8 0.4 copy-done.4
  98.2 2.1 fusion.5
  100.3 0.0 copy-start.5
  100.4 35.1 %all-gather.3.cloned.1.call-done = bf16[384,7168]{1,0:T(8,128)(2,1)} async-done(((bf16[384,1792]{1,0:T(8,128)(2,1)}), bf16[384,7168]{1,0:T(8,128)(2,1)}) %all-gather.3.cloned.1.call-update) | async-done | bytes 5505040 | tf_op jit(solution)/shard_map/all_gather | solution.py:51
  135.4 5.8 %multiply_reduce_fusion = (f32[384]{0:T(512)S(1)}, f32[384,256]{0,1:T(8,128)S(1)}) fusion(f32[384,256]{0,1:T(8,128)S(1)} %fusion.5, f32[384,256]{0,1:T(8,128)S(1)} %fusion.2, bf16[384,7168]{1,0:T(8,128)(2,1)} %all-gather.3.cloned.1.call-done, bf16[1,256,7168]{2,1,0:T(8,128)(2,1)} %param.13), kind=kOutput, calls=%fused_computation.14 | convolution fusion | flops 1409973888 | bytes 10356224 | tf_op jit(solution)/shard_map/dot_general | solution.py:54
  141.2 0.1 all_to_all.23
  141.3 6.5 %psum.7 = f32[8,1,48]{2,1,0:T(1,128)} all-reduce(f32[8,1,48]{2,1,0:T(1,128)S(1)} %all_to_all.23), channel_id=1, replica_groups=mesh['expert'=8,'tensor'=4] {'tensor'}, use_global_device_ids=true, to_apply=%region_7.8 | all-reduce | flops 384 | bytes 3072 | tf_op jit(solution)/shard_map/psum | solution.py:70
  147.8 5.7 %all-to-all-start.4 = ((f32[8,1,48]{2,1,0:T(1,128)}), f32[8,1,48]{2,1,0:T(1,128)S(1)}, u32[]{:S(2)}, u32[]{:S(2)}) async-start(f32[8,1,48]{2,1,0:T(1,128)} %psum.7), calls=%async_computation.5 | async-start | bytes 8192 | tf_op jit(solution)/shard_map/all_to_all | solution.py:81
  153.4 0.0 reduce-scatter.2.cloned.1.call-start
  153.5 0.0 copy-done.5
  153.5 6.3 %all-to-all-done.4 = f32[8,1,48]{2,1,0:T(1,128)S(1)} async-done(((f32[8,1,48]{2,1,0:T(1,128)}), f32[8,1,48]{2,1,0:T(1,128)S(1)}, u32[]{:S(2)}, u32[]{:S(2)}) %all-to-all-start.4) | async-done | bytes 1568 | tf_op jit(solution)/shard_map/all_to_all | solution.py:81
  159.8 0.5 broadcast.43
  160.3 0.7 reduce.9
  161.0 0.1 broadcast_in_dim.30
  161.1 0.7 select_reduce_fusion
  161.8 0.1 convert_element_type.67
  161.9 8.8 %all_to_all.32 = bf16[8,1,48]{2,1,0:T(2,128)(2,1)S(1)} all-to-all(bf16[8,1,48]{2,1,0:T(2,128)(2,1)S(1)} %convert_element_type.67), channel_id=1, replica_groups=mesh['expert'=8,'tensor'=4] {'expert'}, dimensions={0} | all-to-all | bytes 1536 | tf_op jit(solution)/shard_map/all_to_all | solution.py:41
  170.7 0.1 reshape.84
  170.8 4.0 %fusion = f32[384,7168]{1,0:T(8,128)S(1)} fusion(bf16[1,7168,256]{2,1,0:T(8,128)(2,1)} %param.11, f32[384,256]{0,1:T(8,128)S(1)} %fusion.2, f32[384,256]{0,1:T(8,128)S(1)} %fusion.5, f32[384,256]{0,1:T(8,128)S(1)} %get-tuple-element.5, f32[384]{0:T(512)S(1)} %reshape.84), kind=kOutput, calls=%fused_computation.1 | convolution fusion | flops 1410367488 | bytes 15861248 | tf_op jit(solution)/shard_map/dot_general | solution.py:64
  174.8 4.1 %add_convert_fusion = bf16[384,7168]{1,0:T(8,128)(2,1)} fusion(f32[384,7168]{1,0:T(8,128)S(1)} %fusion, bf16[1,7168,256]{2,1,0:T(8,128)(2,1)S(1)} %copy-done.2, f32[384,256]{0,1:T(8,128)S(1)} %get-tuple-element.5, f32[384]{0:T(512)S(1)} %reshape.84, f32[384,256]{0,1:T(8,128)S(1)} %fusion.2), kind=kOutput, calls=%fused_computation | convolution fusion | flops 1415479296 | bytes 20973056 | tf_op jit(solution)/shard_map/dot_general | solution.py:67
  178.9 0.0 reduce-scatter.2.cloned.1.call-update
  178.9 50.5 %reduce-scatter.2.cloned.1.call-done = bf16[384,1792]{1,0:T(8,128)(2,1)} async-done(((bf16[384,7168]{1,0:T(8,128)(2,1)}), bf16[384,1792]{1,0:T(8,128)(2,1)}) %reduce-scatter.2.cloned.1.call-update) | async-done | bytes 1376272 | tf_op jit(solution)/shard_map/reduce_scatter | solution.py:71
  229.4 38.9 %all_to_all.33 = bf16[8,48,1792]{2,1,0:T(8,128)(2,1)S(1)} all-to-all(bf16[8,48,1792]{2,1,0:T(8,128)(2,1)} %bitcast.43), channel_id=1, replica_groups=mesh['expert'=8,'tensor'=4] {'expert'}, dimensions={0} | all-to-all | bytes 2752512 | tf_op jit(solution)/shard_map/all_to_all | solution.py:74
  268.3 1.2 convolution_convert_fusion.2
  (10 shorter events, 0.1 us)
Async XLA Ops:
  7.2 3.1 %copy-start = (bf16[128,1792]{1,0:T(8,128)(2,1)S(1)}, bf16[128,1792]{1,0:T(8,128)(2,1)}, u32[]{:S(2)}) copy-start(bf16[128,1792]{1,0:T(8,128)(2,1)} %param.7) | copy-start | bytes 1376260
  7.2 44.3 %copy-start.3 = (bf16[128,1792]{1,0:T(8,128)(2,1)S(1)}, bf16[128,1792]{1,0:T(8,128)(2,1)}, u32[]{:S(2)}) copy-start(bf16[128,1792]{1,0:T(8,128)(2,1)} %param.8) | copy-start | bytes 1376260
  7.2 84.7 %all-gather.5.cloned.1.call-start = ((), (), s32[]{:S(2)}) async-start(), calls=%async_computation.7 | async-start | bytes 6881280 | tf_op jit(solution)/shard_map/all_gather | solution.py:50
  51.4 84.0 %all-gather.3.cloned.1.call-start = ((), (), s32[]{:S(2)}) async-start(), calls=%async_computation.6 | async-start | bytes 6881280 | tf_op jit(solution)/shard_map/all_gather | solution.py:51
  91.9 5.9 %copy-start.1 = (bf16[1,7168,256]{2,1,0:T(8,128)(2,1)S(1)}, bf16[1,7168,256]{2,1,0:T(8,128)(2,1)}, u32[]{:S(2)}) copy-start(bf16[1,7168,256]{2,1,0:T(8,128)(2,1)} %param.12) | copy-start | bytes 11010052
  91.9 6.3 %copy-start.4 = (bf16[384,7168]{1,0:T(8,128)(2,1)S(1)}, bf16[384,7168]{1,0:T(8,128)(2,1)}, u32[]{:S(2)}) copy-start(bf16[384,7168]{1,0:T(8,128)(2,1)} %all-gather.5.cloned.1.call-done) | copy-start | bytes 16515076
  100.3 53.1 %copy-start.5 = (bf16[128,2]{0,1:T(2,128)(2,1)S(1)}, bf16[128,2]{0,1:T(2,128)(2,1)}, u32[]{:S(2)}) copy-start(bf16[128,2]{0,1:T(2,128)(2,1)} %param.10) | copy-start | bytes 1540
  147.8 12.1 %all-to-all-start.4 = ((f32[8,1,48]{2,1,0:T(1,128)}), f32[8,1,48]{2,1,0:T(1,128)S(1)}, u32[]{:S(2)}, u32[]{:S(2)}) async-start(f32[8,1,48]{2,1,0:T(1,128)} %psum.7), calls=%async_computation.5 | async-start | bytes 8192 | tf_op jit(solution)/shard_map/all_to_all | solution.py:81
  153.4 76.0 %reduce-scatter.2.cloned.1.call-start = ((), (), s32[]{:S(2)}) async-start(), calls=%async_computation.8 | async-start | bytes 6881280 | tf_op jit(solution)/shard_map/reduce_scatter | solution.py:71
  170.8 4.0 %copy-start.2 = (bf16[1,7168,256]{2,1,0:T(8,128)(2,1)S(1)}, bf16[1,7168,256]{2,1,0:T(8,128)(2,1)}, u32[]{:S(2)}) copy-start(bf16[1,7168,256]{2,1,0:T(8,128)(2,1)} %param.12) | copy-start | bytes 11010052
Sparse Core Ops, SparseCore 0:
  51.6 40.2 all-gather.4
  93.4 41.9 all-gather.2
  179.0 50.3 reduce-scatter.1
where the time goes:
time: 276 us
  blocking collectives  131 us (47%)
  waiting for transfers between devices  95.7 us (35%)
  matrix products  24.1 us (9%)
  between operations  13.9 us (5%)
  starting transfers between devices  5.8 us (2%)
  other arithmetic  2.86 us (1%)
  local copies, waits for them, and re-layouts  2.84 us (1%)
    reduce_scatter x1, waiting for transfers between devices, local(): lax.psum_scatter(contrib.astype(jnp.bfloat16), 'tensor', scatter_dimensio...  50.5 us
    all_to_all x1, blocking collectives, local(): lax.all_to_all(send_x.reshape(n_experts, most_slots, quarter), 'expert',...  40.6 us
    all_to_all x1, blocking collectives, local(): lax.all_to_all(shares.reshape(n_experts, most_slots, quarter), 'expert',...  38.9 us
    all_to_all x1, blocking collectives, local(): lax.all_to_all(send_dy.reshape(n_experts, most_slots, quarter), 'expert',...  36.1 us
    all_gather x1, waiting for transfers between devices, local(): piece_dy = lax.all_gather(rows_dy, 'tensor', axis=1, tiled=True)  35.1 us
    all_to_all x1, blocking collectives, local(): lax.all_to_all(send_g.reshape(n_experts, most_slots), 'expert', split_axi...  8.82 us
    psum x1, blocking collectives, local(): slot_grad = lax.psum(partial_grad, 'tensor')  6.49 us
    all_to_all x1, waiting for transfers between devices, local(): lax.all_to_all(slot_grad.reshape(n_experts, most_slots), 'expert', split_...  6.32 us
  transfers between devices with their start and end apart: 4, of which 4 were waited for; matrix products, arithmetic and copies ran while one was open for 3% of the time, Pallas kernels for 0%

commit v1 on v0

--- a/solution.py
+++ b/solution.py
@@ -47,8 +47,8 @@
     gate_mat = w_gate[0]
     up_mat = w_up[0]
     down_mat = w_down[0]
-    piece_x = lax.all_gather(rows_x, "tensor", axis=1, tiled=True)
-    piece_dy = lax.all_gather(rows_dy, "tensor", axis=1, tiled=True)
+    passed = lax.all_gather(jnp.concatenate([rows_x, rows_dy], 0), "tensor", tiled=True, axis=1)
+    piece_x, piece_dy = jnp.split(passed, [rows_x.shape[0]], 0)
     pre_sum = jnp.dot(piece_x, gate_mat, preferred_element_type=jnp.float32)
     up_sum = jnp.dot(piece_x, up_mat, preferred_element_type=jnp.float32)
     grad_sum = lax.dot_general(

time: 276 us -> 311 us (1.13)
  waiting for transfers between devices: 95.7 us -> 160 us
  blocking collectives: 131 us -> 91.2 us
  starting transfers between devices: 5.8 us -> 13 us
    all_to_all x1 -> x0, blocking collectives: 36.1 us -> none  [local(): lax.all_to_all(send_dy.reshape(n_experts, most_slots, quarter), 'expert',...]
    all_gather x2 -> x1, waiting for transfers between devices: 38.8 us -> 71.7 us  [local(): lax.all_gather(jnp.concatenate([rows_x, rows_dy], 0), 'tensor', tiled=Tru...]
    all_to_all x0 -> x1, waiting for transfers between devices: none -> 31.2 us  [local(): lax.all_to_all(send_dy.reshape(n_experts, most_slots, quarter), 'expert',...]
    all_to_all x0 -> x1, starting transfers between devices: none -> 7.28 us  [local(): lax.all_to_all(send_dy.reshape(n_experts, most_slots, quarter), 'expert',...]
    dot_general x1, matrix products: 5.76 us -> 2.09 us  [local(): lax.dot_general(piece_dy, down_mat, (((1,), (1,)), ((), ())), preferred_e...]
    all_to_all x1, blocking collectives: 40.6 us -> 37 us  [local(): lax.all_to_all(send_x.reshape(n_experts, most_slots, quarter), 'expert',...]
  transfers between devices with their start and end apart: 4 -> 4, of which waited for: 4 -> 4; matrix products, arithmetic and copies ran while one was open for 3% -> 0% of each run, Pallas kernels for 0% -> 0%
where the time goes in v1:
time: 311 us
  waiting for transfers between devices  160 us (51%)
  blocking collectives  91.2 us (29%)
  matrix products  25.3 us (8%)
  between operations  14.2 us (5%)
  starting transfers between devices  13 us (4%)
  other arithmetic  4.66 us (1%)
    all_gather x1, waiting for transfers between devices, local(): lax.all_gather(jnp.concatenate([rows_x, rows_dy], 0), 'tensor', tiled=Tru...  71.7 us
    reduce_scatter x1, waiting for transfers between devices, local(): lax.psum_scatter(contrib.astype(jnp.bfloat16), 'tensor', scatter_dimensio...  50.5 us
    all_to_all x1, blocking collectives, local(): lax.all_to_all(shares.reshape(n_experts, most_slots, quarter), 'expert',...  38.9 us
    all_to_all x1, blocking collectives, local(): lax.all_to_all(send_x.reshape(n_experts, most_slots, quarter), 'expert',...  37 us
    all_to_all x1, waiting for transfers between devices, local(): lax.all_to_all(send_dy.reshape(n_experts, most_slots, quarter), 'expert',...  31.2 us
    all_to_all x1, blocking collectives, local(): lax.all_to_all(send_g.reshape(n_experts, most_slots), 'expert', split_axi...  8.82 us
    all_to_all x1, starting transfers between devices, local(): lax.all_to_all(send_dy.reshape(n_experts, most_slots, quarter), 'expert',...  7.28 us
    psum x1, blocking collectives, local(): slot_grad = lax.psum(partial_grad, 'tensor')  6.5 us
  transfers between devices with their start and end apart: 4, of which 4 were waited for; matrix products, arithmetic and copies ran while one was open for 0% of the time, Pallas kernels for 0%

profile of v1, /device:TPU:0, one launch (start us, length us, event | category | flops | bytes accessed | tf_op | source)
XLA Modules:
  0.0 310.7 jit_solution(4444639944998616836)
XLA Ops:
  7.2 0.0 copy-start
  7.2 0.8 copy.28
  8.0 0.1 eq.42
  8.2 0.1 eq.38
  8.3 0.6 reduce-window.6
  8.9 0.2 slice_reduce_fusion
  9.2 0.1 fusion.19
  9.2 0.1 reduce_sum.39
  9.4 0.1 copy.30
  9.5 0.7 multiply_add_fusion
  10.2 0.0 copy-done
  10.2 1.6 convolution_convert_fusion
  11.8 7.3 %all-to-all-start.2 = ((bf16[8,48,1792]{2,1,0:T(8,128)(2,1)}), bf16[8,48,1792]{2,1,0:T(8,128)(2,1)S(1)}, u32[]{:S(2)}, u32[]{:S(2)}) async-start(bf16[8,48,1792]{2,1,0:T(8,128)(2,1)} %bitcast.4), calls=%async_computation.2 | async-start | bytes 2752512 | tf_op jit(solution)/shard_map/all_to_all | solution.py:34
  19.1 0.0 all-gather.2.cloned.1.call-start
  19.1 1.5 convolution_convert_fusion.1
  20.7 31.2 %all-to-all-done.2 = bf16[8,48,1792]{2,1,0:T(8,128)(2,1)S(1)} async-done(((bf16[8,48,1792]{2,1,0:T(8,128)(2,1)}), bf16[8,48,1792]{2,1,0:T(8,128)(2,1)S(1)}, u32[]{:S(2)}, u32[]{:S(2)}) %all-to-all-start.2) | async-done | bytes 1376288 | tf_op jit(solution)/shard_map/all_to_all | solution.py:34
  51.9 37.0 %all_to_all.30 = bf16[8,48,1792]{2,1,0:T(8,128)(2,1)S(1)} all-to-all(bf16[8,48,1792]{2,1,0:T(8,128)(2,1)S(1)} %bitcast.36), channel_id=1, replica_groups=mesh['expert'=8,'tensor'=4] {'expert'}, dimensions={0} | all-to-all | bytes 2752512 | tf_op jit(solution)/shard_map/all_to_all | solution.py:27
  88.9 1.8 pad_maximum_fusion
  90.7 0.0 all-gather.2.cloned.1.call-update
  90.7 71.7 %all-gather.2.cloned.1.call-done = bf16[768,7168]{1,0:T(8,128)(2,1)} async-done(((bf16[768,1792]{1,0:T(8,128)(2,1)}), bf16[768,7168]{1,0:T(8,128)(2,1)}) %all-gather.2.cloned.1.call-update) | async-done | bytes 11010064 | tf_op jit(solution)/shard_map/all_gather | solution.py:50
  162.5 5.9 %fusion.2 = f32[384,256]{0,1:T(8,128)S(1)} fusion(bf16[768,7168]{1,0:T(8,128)(2,1)} %all-gather.2.cloned.1.call-done, bf16[1,7168,256]{2,1,0:T(8,128)(2,1)} %param.11), kind=kOutput, calls=%fused_computation.3 | convolution fusion | flops 1409286144 | bytes 9568256 | tf_op jit(solution)/shard_map/dot_general | solution.py:52
  168.4 0.0 slice-start.2
  168.4 0.0 copy-start.3
  168.4 4.9 %fusion.4 = f32[384,256]{0,1:T(8,128)S(1)} fusion(bf16[768,7168]{1,0:T(8,128)(2,1)} %all-gather.2.cloned.1.call-done, bf16[1,7168,256]{2,1,0:T(8,128)(2,1)S(1)} %copy-done.1), kind=kOutput, calls=%fused_computation.5 | convolution fusion | flops 1409286144 | bytes 9568256 | tf_op jit(solution)/shard_map/dot_general | solution.py:53
  173.3 0.0 slice-done
  173.4 0.0 slice-done.1
  173.4 0.0 slice-done.2
  173.4 0.0 copy-done.3
  173.4 0.0 copy-start.4
  173.4 2.1 multiply_reduce_fusion
  175.5 0.1 all_to_all.23
  175.6 6.5 %psum.7 = f32[8,1,48]{2,1,0:T(1,128)} all-reduce(f32[8,1,48]{2,1,0:T(1,128)S(1)} %all_to_all.23), channel_id=1, replica_groups=mesh['expert'=8,'tensor'=4] {'tensor'}, use_global_device_ids=true, to_apply=%region_7.8 | all-reduce | flops 384 | bytes 3072 | tf_op jit(solution)/shard_map/psum | solution.py:70
  182.1 5.7 %all-to-all-start.4 = ((f32[8,1,48]{2,1,0:T(1,128)}), f32[8,1,48]{2,1,0:T(1,128)S(1)}, u32[]{:S(2)}, u32[]{:S(2)}) async-start(f32[8,1,48]{2,1,0:T(1,128)} %psum.7), calls=%async_computation.5 | async-start | bytes 8192 | tf_op jit(solution)/shard_map/all_to_all | solution.py:81
  187.8 0.0 reduce-scatter.2.cloned.1.call-start
  187.8 6.3 %all-to-all-done.4 = f32[8,1,48]{2,1,0:T(1,128)S(1)} async-done(((f32[8,1,48]{2,1,0:T(1,128)}), f32[8,1,48]{2,1,0:T(1,128)S(1)}, u32[]{:S(2)}, u32[]{:S(2)}) %all-to-all-start.4) | async-done | bytes 1568 | tf_op jit(solution)/shard_map/all_to_all | solution.py:81
  194.2 0.5 broadcast.43
  194.7 0.7 reduce.9
  195.3 0.1 broadcast_in_dim.30
  195.4 0.7 select_reduce_fusion
  196.1 0.1 convert_element_type.67
  196.2 8.8 %all_to_all.31 = bf16[8,1,48]{2,1,0:T(2,128)(2,1)S(1)} all-to-all(bf16[8,1,48]{2,1,0:T(2,128)(2,1)S(1)} %convert_element_type.67), channel_id=1, replica_groups=mesh['expert'=8,'tensor'=4] {'expert'}, dimensions={0} | all-to-all | bytes 1536 | tf_op jit(solution)/shard_map/all_to_all | solution.py:41
  205.1 0.1 reshape.84
  205.1 4.0 %fusion.6 = f32[384,7168]{1,0:T(8,128)S(1)} fusion(bf16[1,7168,256]{2,1,0:T(8,128)(2,1)} %param.11, f32[384,256]{0,1:T(8,128)S(1)} %fusion.2, f32[384,256]{0,1:T(8,128)S(1)} %fusion.4, f32[384,256]{0,1:T(8,128)S(1)} %get-tuple-element.5, f32[384]{0:T(512)S(1)} %reshape.84), kind=kOutput, calls=%fused_computation.7 | convolution fusion | flops 1410367488 | bytes 15861248 | tf_op jit(solution)/shard_map/dot_general | solution.py:64
  209.1 4.1 %add_convert_fusion = bf16[384,7168]{1,0:T(8,128)(2,1)} fusion(f32[384,7168]{1,0:T(8,128)S(1)} %fusion.6, bf16[1,7168,256]{2,1,0:T(8,128)(2,1)S(1)} %copy-done.2, f32[384,256]{0,1:T(8,128)S(1)} %get-tuple-element.5, f32[384]{0:T(512)S(1)} %reshape.84, f32[384,256]{0,1:T(8,128)S(1)} %fusion.2), kind=kOutput, calls=%fused_computation | convolution fusion | flops 1415479296 | bytes 20973056 | tf_op jit(solution)/shard_map/dot_general | solution.py:67
  213.2 0.0 reduce-scatter.2.cloned.1.call-update
  213.2 50.5 %reduce-scatter.2.cloned.1.call-done = bf16[384,1792]{1,0:T(8,128)(2,1)} async-done(((bf16[384,7168]{1,0:T(8,128)(2,1)}), bf16[384,1792]{1,0:T(8,128)(2,1)}) %reduce-scatter.2.cloned.1.call-update) | async-done | bytes 1376272 | tf_op jit(solution)/shard_map/reduce_scatter | solution.py:71
  263.7 38.9 %all_to_all.32 = bf16[8,48,1792]{2,1,0:T(8,128)(2,1)S(1)} all-to-all(bf16[8,48,1792]{2,1,0:T(8,128)(2,1)} %bitcast.39), channel_id=1, replica_groups=mesh['expert'=8,'tensor'=4] {'expert'}, dimensions={0} | all-to-all | bytes 2752512 | tf_op jit(solution)/shard_map/all_to_all | solution.py:74
  302.7 1.2 convolution_convert_fusion.2
  (14 shorter events, 0.1 us)
Async XLA Ops:
  7.2 3.1 copy-start
  11.8 40.1 %all-to-all-start.2 = ((bf16[8,48,1792]{2,1,0:T(8,128)(2,1)}), bf16[8,48,1792]{2,1,0:T(8,128)(2,1)S(1)}, u32[]{:S(2)}, u32[]{:S(2)}) async-start(bf16[8,48,1792]{2,1,0:T(8,128)(2,1)} %bitcast.4), calls=%async_computation.2 | async-start | bytes 2752512 | tf_op jit(solution)/shard_map/all_to_all | solution.py:34
  19.1 143.4 %all-gather.2.cloned.1.call-start = ((), (), s32[]{:S(2)}) async-start(), calls=%async_computation.6 | async-start | bytes 13762560 | tf_op jit(solution)/shard_map/all_gather | solution.py:50
  162.5 5.9 %copy-start.1 = (bf16[1,7168,256]{2,1,0:T(8,128)(2,1)S(1)}, bf16[1,7168,256]{2,1,0:T(8,128)(2,1)}, u32[]{:S(2)}) copy-start(bf16[1,7168,256]{2,1,0:T(8,128)(2,1)} %param.12) | copy-start | bytes 11010052
  162.5 10.9 %slice-start = ((s8[11010048]{0:T(1024)(128)(4,1)}), s8[4194304]{0:T(1024)(128)(4,1)S(1)}, s32[]{:S(2)}) async-start(s8[11010048]{0:T(1024)(128)(4,1)} %bitcast.40), calls=%async_computation.8 | async-start | bytes 8388608
  162.5 10.9 %slice-start.1 = ((s8[11010048]{0:T(1024)(128)(4,1)}), s8[4194304]{0:T(1024)(128)(4,1)S(1)}, s32[]{:S(2)}) async-start(s8[11010048]{0:T(1024)(128)(4,1)} %bitcast.40), calls=%async_computation.9 | async-start | bytes 8388608
  168.4 5.0 %slice-start.2 = ((s8[11010048]{0:T(1024)(128)(4,1)}), s8[2621440]{0:T(1024)(128)(4,1)S(1)}, s32[]{:S(2)}) async-start(s8[11010048]{0:T(1024)(128)(4,1)} %bitcast.40), calls=%async_computation.10 | async-start | bytes 5242880
  168.4 5.0 %copy-start.3 = (bf16[1,256,7168]{2,1,0:T(8,128)(2,1)S(1)}, bf16[1,256,7168]{2,1,0:T(8,128)(2,1)}, u32[]{:S(2)}) copy-start(bf16[1,256,7168]{2,1,0:T(8,128)(2,1)} %param.13) | copy-start | bytes 11010052
  173.4 14.4 %copy-start.4 = (bf16[128,2]{0,1:T(2,128)(2,1)S(1)}, bf16[128,2]{0,1:T(2,128)(2,1)}, u32[]{:S(2)}) copy-start(bf16[128,2]{0,1:T(2,128)(2,1)} %param.10) | copy-start | bytes 1540
  182.1 12.1 %all-to-all-start.4 = ((f32[8,1,48]{2,1,0:T(1,128)}), f32[8,1,48]{2,1,0:T(1,128)S(1)}, u32[]{:S(2)}, u32[]{:S(2)}) async-start(f32[8,1,48]{2,1,0:T(1,128)} %psum.7), calls=%async_computation.5 | async-start | bytes 8192 | tf_op jit(solution)/shard_map/all_to_all | solution.py:81
  187.8 76.0 %reduce-scatter.2.cloned.1.call-start = ((), (), s32[]{:S(2)}) async-start(), calls=%async_computation.7 | async-start | bytes 6881280 | tf_op jit(solution)/shard_map/reduce_scatter | solution.py:71
  205.1 4.0 %copy-start.2 = (bf16[1,7168,256]{2,1,0:T(8,128)(2,1)S(1)}, bf16[1,7168,256]{2,1,0:T(8,128)(2,1)}, u32[]{:S(2)}) copy-start(bf16[1,7168,256]{2,1,0:T(8,128)(2,1)} %param.12) | copy-start | bytes 11010052
Sparse Core Ops, SparseCore 0:
  90.8 71.5 all-gather.1
  213.4 50.3 reduce-scatter.1
